TPU v7x, 256 devices: a whole 4x4x8 slice. The times are simulated.
256 devices in a mesh: rows: 16 (over z, core), feat: 16 (over x, y).
Axes of the slice: x: 4, y: 4, z: 8, core: 2. Of those that a mesh axis runs over, the one named last changes fastest.
Arguments:
- features: bfloat16 [16384, 16384], P('rows', 'feat'), may hold values from -0.046875 to 0.046875
- inverse_gram: float32 [16384, 1024], P('feat'), as said below
- targets: float32 [128, 16384], P('feat', 'rows'), may hold values from -6 to 6
Outputs:
- weights: float32 [128, 16384], P(None, 'feat')
- residual: float32 [128, 16384], P('feat', 'rows')
Inputs may be any that keep to these rules, and one draw needn't show every extreme that they name: Each block of inverse_gram is symmetric.
All inputs are finite; a program needn't handle non-finite values.
Results may differ from a plain program's by a relative error of at most 0.007.
Values sent between devices are 32-bit elements; how exact they have to be, the bound alone decides.
No kernel may reach another device: no remote copies, remote signals or barrier semaphores. Data moves between devices by JAX's collectives and lax.ppermute only.
A program may use at most 64 MiB of HBM per device.

v0:
```python
import jax
import jax.numpy as jnp
from jax import lax
from jax.sharding import PartitionSpec as P

TGT = 128
TURNS = 2
ridge_weight = 0.5


def passed_along(block, axis, distance):
    devices = range(lax.axis_size(axis))
    route = [((i - distance) % len(devices), i) for i in devices]
    return lax.ppermute(block, axis, route)


def local(features, inverse_gram, targets):
    block_count = lax.axis_size("feat")
    position = lax.axis_index("feat")
    panel_width = targets.shape[0]

    def refine(panel_rows, panel_weights):
        partial_value = jnp.dot(
            panel_rows.astype(jnp.bfloat16), features, preferred_element_type=jnp.float32
        )
        projection = lax.psum(partial_value, "rows")
        increment = jnp.dot(
            projection - ridge_weight * panel_weights, inverse_gram, precision=lax.Precision.HIGHEST
        )
        fitted = lax.dot_general(
            increment.astype(jnp.bfloat16),
            features,
            (((1,), (1,)), ((), ())),
            preferred_element_type=jnp.float32,
        )
        return (panel_rows - fitted, panel_weights + increment)

    def advance(section, carried):
        residual, weights = carried
        panel_index = (position - section) % block_count
        start = panel_index * panel_width
        panel_weights = lax.dynamic_slice_in_dim(weights, start, panel_width, 0)
        residual, panel_weights = refine(residual, panel_weights)
        weights = lax.dynamic_update_slice_in_dim(weights, panel_weights, start, 0)
        residual = passed_along(residual, "feat", 1)
        return (residual, weights)

    carried = (targets, jnp.zeros((TGT, features.shape[1]), jnp.float32))
    for sweep_index in range(TURNS):
        offset = sweep_index * block_count

        def sweep_step(inner, state, offset=offset):
            return advance(inner + offset, state)

        carried = lax.fori_loop(0, block_count, sweep_step, carried)
    residual, weights = carried
    return (weights, residual)


def solution(mesh):
    placed = (P("rows", "feat"), P("feat", None), P("feat", "rows"))
    return jax.shard_map(
        local,
        mesh=mesh,
        in_specs=placed,
        out_specs=(P(None, "feat"), P("feat", "rows")),
        check_vma=False,
    )
```

profile of v0, /device:TPU:0, one launch (start us, length us, event | category | flops | bytes accessed | tf_op | source)
XLA Modules:
  0.0 1925.4 jit_solution(16532286769631520528)
XLA Ops:
  1.4 963.3 %while.34 = (s32[]{:T(128)}, f32[8,1024]{1,0:T(8,128)S(1)}, f32[128,1024]{1,0:T(8,128)S(1)}, bf16[1024,1024]{1,0:T(8,128)(2,1)}, s32[]{:T(128)}, /*index=5*/f32[...) while((s32[]{:T(128)}, f32[8,1024]{1,0:T(8,128)S(1)}, ...), condition=%wide.region_2.3_spmd, body=%wide.region_0.2_spmd.sunk | while | flops 134275072 | bytes 17334632 | solution.py:55
  3.4 49.1 %psum.30 = f32[8,1024]{1,0:T(8,128)S(1)} all-reduce(f32[8,1024]{1,0:T(8,128)S(1)} %fusion.48), channel_id=1, replica_groups=mesh['rows'=16,'feat'=16] {'rows'}, use_global_device_ids=true, to_apply=%region_1.1 | all-reduce | flops 8192 | bytes 65536 | tf_op jit(solution)/shard_map/while/body/eval_jaxpr/psum | solution.py:26
  66.9 45.7 %psum.30 = f32[8,1024]{1,0:T(8,128)S(1)} all-reduce(f32[8,1024]{1,0:T(8,128)S(1)} %fusion.48), channel_id=1, replica_groups=mesh['rows'=16,'feat'=16] {'rows'}, use_global_device_ids=true, to_apply=%region_1.1 | all-reduce | flops 8192 | bytes 65536 | tf_op jit(solution)/shard_map/while/body/eval_jaxpr/psum | solution.py:26
  117.7 7.2 collective-permute-done
  126.9 45.7 %psum.30 = f32[8,1024]{1,0:T(8,128)S(1)} all-reduce(f32[8,1024]{1,0:T(8,128)S(1)} %fusion.48), channel_id=1, replica_groups=mesh['rows'=16,'feat'=16] {'rows'}, use_global_device_ids=true, to_apply=%region_1.1 | all-reduce | flops 8192 | bytes 65536 | tf_op jit(solution)/shard_map/while/body/eval_jaxpr/psum | solution.py:26
  177.7 7.2 collective-permute-done
  186.9 45.7 %psum.30 = f32[8,1024]{1,0:T(8,128)S(1)} all-reduce(f32[8,1024]{1,0:T(8,128)S(1)} %fusion.48), channel_id=1, replica_groups=mesh['rows'=16,'feat'=16] {'rows'}, use_global_device_ids=true, to_apply=%region_1.1 | all-reduce | flops 8192 | bytes 65536 | tf_op jit(solution)/shard_map/while/body/eval_jaxpr/psum | solution.py:26
  237.7 7.2 collective-permute-done
  246.9 45.7 %psum.30 = f32[8,1024]{1,0:T(8,128)S(1)} all-reduce(f32[8,1024]{1,0:T(8,128)S(1)} %fusion.48), channel_id=1, replica_groups=mesh['rows'=16,'feat'=16] {'rows'}, use_global_device_ids=true, to_apply=%region_1.1 | all-reduce | flops 8192 | bytes 65536 | tf_op jit(solution)/shard_map/while/body/eval_jaxpr/psum | solution.py:26
  297.7 7.2 collective-permute-done
  306.8 45.7 %psum.30 = f32[8,1024]{1,0:T(8,128)S(1)} all-reduce(f32[8,1024]{1,0:T(8,128)S(1)} %fusion.48), channel_id=1, replica_groups=mesh['rows'=16,'feat'=16] {'rows'}, use_global_device_ids=true, to_apply=%region_1.1 | all-reduce | flops 8192 | bytes 65536 | tf_op jit(solution)/shard_map/while/body/eval_jaxpr/psum | solution.py:26
  357.6 7.2 collective-permute-done
  366.8 45.7 %psum.30 = f32[8,1024]{1,0:T(8,128)S(1)} all-reduce(f32[8,1024]{1,0:T(8,128)S(1)} %fusion.48), channel_id=1, replica_groups=mesh['rows'=16,'feat'=16] {'rows'}, use_global_device_ids=true, to_apply=%region_1.1 | all-reduce | flops 8192 | bytes 65536 | tf_op jit(solution)/shard_map/while/body/eval_jaxpr/psum | solution.py:26
  417.6 7.2 collective-permute-done
  426.8 45.7 %psum.30 = f32[8,1024]{1,0:T(8,128)S(1)} all-reduce(f32[8,1024]{1,0:T(8,128)S(1)} %fusion.48), channel_id=1, replica_groups=mesh['rows'=16,'feat'=16] {'rows'}, use_global_device_ids=true, to_apply=%region_1.1 | all-reduce | flops 8192 | bytes 65536 | tf_op jit(solution)/shard_map/while/body/eval_jaxpr/psum | solution.py:26
  477.6 7.2 collective-permute-done
  486.8 45.7 %psum.30 = f32[8,1024]{1,0:T(8,128)S(1)} all-reduce(f32[8,1024]{1,0:T(8,128)S(1)} %fusion.48), channel_id=1, replica_groups=mesh['rows'=16,'feat'=16] {'rows'}, use_global_device_ids=true, to_apply=%region_1.1 | all-reduce | flops 8192 | bytes 65536 | tf_op jit(solution)/shard_map/while/body/eval_jaxpr/psum | solution.py:26
  537.6 7.2 collective-permute-done
  546.8 45.7 %psum.30 = f32[8,1024]{1,0:T(8,128)S(1)} all-reduce(f32[8,1024]{1,0:T(8,128)S(1)} %fusion.48), channel_id=1, replica_groups=mesh['rows'=16,'feat'=16] {'rows'}, use_global_device_ids=true, to_apply=%region_1.1 | all-reduce | flops 8192 | bytes 65536 | tf_op jit(solution)/shard_map/while/body/eval_jaxpr/psum | solution.py:26
  597.6 7.2 collective-permute-done
  606.8 45.7 %psum.30 = f32[8,1024]{1,0:T(8,128)S(1)} all-reduce(f32[8,1024]{1,0:T(8,128)S(1)} %fusion.48), channel_id=1, replica_groups=mesh['rows'=16,'feat'=16] {'rows'}, use_global_device_ids=true, to_apply=%region_1.1 | all-reduce | flops 8192 | bytes 65536 | tf_op jit(solution)/shard_map/while/body/eval_jaxpr/psum | solution.py:26
  657.6 7.2 collective-permute-done
  666.8 45.7 %psum.30 = f32[8,1024]{1,0:T(8,128)S(1)} all-reduce(f32[8,1024]{1,0:T(8,128)S(1)} %fusion.48), channel_id=1, replica_groups=mesh['rows'=16,'feat'=16] {'rows'}, use_global_device_ids=true, to_apply=%region_1.1 | all-reduce | flops 8192 | bytes 65536 | tf_op jit(solution)/shard_map/while/body/eval_jaxpr/psum | solution.py:26
  717.6 7.2 collective-permute-done
  726.8 45.7 %psum.30 = f32[8,1024]{1,0:T(8,128)S(1)} all-reduce(f32[8,1024]{1,0:T(8,128)S(1)} %fusion.48), channel_id=1, replica_groups=mesh['rows'=16,'feat'=16] {'rows'}, use_global_device_ids=true, to_apply=%region_1.1 | all-reduce | flops 8192 | bytes 65536 | tf_op jit(solution)/shard_map/while/body/eval_jaxpr/psum | solution.py:26
  777.6 7.2 collective-permute-done
  786.8 45.7 %psum.30 = f32[8,1024]{1,0:T(8,128)S(1)} all-reduce(f32[8,1024]{1,0:T(8,128)S(1)} %fusion.48), channel_id=1, replica_groups=mesh['rows'=16,'feat'=16] {'rows'}, use_global_device_ids=true, to_apply=%region_1.1 | all-reduce | flops 8192 | bytes 65536 | tf_op jit(solution)/shard_map/while/body/eval_jaxpr/psum | solution.py:26
  837.6 7.2 collective-permute-done
  846.7 45.7 %psum.30 = f32[8,1024]{1,0:T(8,128)S(1)} all-reduce(f32[8,1024]{1,0:T(8,128)S(1)} %fusion.48), channel_id=1, replica_groups=mesh['rows'=16,'feat'=16] {'rows'}, use_global_device_ids=true, to_apply=%region_1.1 | all-reduce | flops 8192 | bytes 65536 | tf_op jit(solution)/shard_map/while/body/eval_jaxpr/psum | solution.py:26
  897.5 7.2 collective-permute-done
  906.7 45.7 %psum.30 = f32[8,1024]{1,0:T(8,128)S(1)} all-reduce(f32[8,1024]{1,0:T(8,128)S(1)} %fusion.48), channel_id=1, replica_groups=mesh['rows'=16,'feat'=16] {'rows'}, use_global_device_ids=true, to_apply=%region_1.1 | all-reduce | flops 8192 | bytes 65536 | tf_op jit(solution)/shard_map/while/body/eval_jaxpr/psum | solution.py:26
  957.5 7.2 collective-permute-done
  964.8 959.8 %while.35 = (s32[]{:T(128)}, f32[8,1024]{1,0:T(8,128)S(1)}, f32[128,1024]{1,0:T(8,128)S(1)}, bf16[1024,1024]{1,0:T(8,128)(2,1)}, s32[]{:T(128)}, /*index=5*/f32[...) while((s32[]{:T(128)}, f32[8,1024]{1,0:T(8,128)S(1)}, ...), condition=%wide.region_5.6_spmd, body=%wide.region_3.5_spmd.sunk | while | flops 134275072 | bytes 17334644 | solution.py:55
  966.7 45.7 %psum.31 = f32[8,1024]{1,0:T(8,128)S(1)} all-reduce(f32[8,1024]{1,0:T(8,128)S(1)} %fusion.56), channel_id=1, replica_groups=mesh['rows'=16,'feat'=16] {'rows'}, use_global_device_ids=true, to_apply=%region_4.4 | all-reduce | flops 8192 | bytes 65536 | tf_op jit(solution)/shard_map/while/body/eval_jaxpr/psum | solution.py:26
  1017.5 7.2 collective-permute-done.1
  1026.7 45.7 %psum.31 = f32[8,1024]{1,0:T(8,128)S(1)} all-reduce(f32[8,1024]{1,0:T(8,128)S(1)} %fusion.56), channel_id=1, replica_groups=mesh['rows'=16,'feat'=16] {'rows'}, use_global_device_ids=true, to_apply=%region_4.4 | all-reduce | flops 8192 | bytes 65536 | tf_op jit(solution)/shard_map/while/body/eval_jaxpr/psum | solution.py:26
  1077.5 7.2 collective-permute-done.1
  1086.7 45.7 %psum.31 = f32[8,1024]{1,0:T(8,128)S(1)} all-reduce(f32[8,1024]{1,0:T(8,128)S(1)} %fusion.56), channel_id=1, replica_groups=mesh['rows'=16,'feat'=16] {'rows'}, use_global_device_ids=true, to_apply=%region_4.4 | all-reduce | flops 8192 | bytes 65536 | tf_op jit(solution)/shard_map/while/body/eval_jaxpr/psum | solution.py:26
  1137.5 7.2 collective-permute-done.1
  1146.7 45.7 %psum.31 = f32[8,1024]{1,0:T(8,128)S(1)} all-reduce(f32[8,1024]{1,0:T(8,128)S(1)} %fusion.56), channel_id=1, replica_groups=mesh['rows'=16,'feat'=16] {'rows'}, use_global_device_ids=true, to_apply=%region_4.4 | all-reduce | flops 8192 | bytes 65536 | tf_op jit(solution)/shard_map/while/body/eval_jaxpr/psum | solution.py:26
  1197.5 7.2 collective-permute-done.1
  1206.7 45.7 %psum.31 = f32[8,1024]{1,0:T(8,128)S(1)} all-reduce(f32[8,1024]{1,0:T(8,128)S(1)} %fusion.56), channel_id=1, replica_groups=mesh['rows'=16,'feat'=16] {'rows'}, use_global_device_ids=true, to_apply=%region_4.4 | all-reduce | flops 8192 | bytes 65536 | tf_op jit(solution)/shard_map/while/body/eval_jaxpr/psum | solution.py:26
  1257.5 7.2 collective-permute-done.1
  1266.7 45.7 %psum.31 = f32[8,1024]{1,0:T(8,128)S(1)} all-reduce(f32[8,1024]{1,0:T(8,128)S(1)} %fusion.56), channel_id=1, replica_groups=mesh['rows'=16,'feat'=16] {'rows'}, use_global_device_ids=true, to_apply=%region_4.4 | all-reduce | flops 8192 | bytes 65536 | tf_op jit(solution)/shard_map/while/body/eval_jaxpr/psum | solution.py:26
  1317.5 7.2 collective-permute-done.1
  1326.7 45.7 %psum.31 = f32[8,1024]{1,0:T(8,128)S(1)} all-reduce(f32[8,1024]{1,0:T(8,128)S(1)} %fusion.56), channel_id=1, replica_groups=mesh['rows'=16,'feat'=16] {'rows'}, use_global_device_ids=true, to_apply=%region_4.4 | all-reduce | flops 8192 | bytes 65536 | tf_op jit(solution)/shard_map/while/body/eval_jaxpr/psum | solution.py:26
  1377.5 7.2 collective-permute-done.1
  1386.7 45.7 %psum.31 = f32[8,1024]{1,0:T(8,128)S(1)} all-reduce(f32[8,1024]{1,0:T(8,128)S(1)} %fusion.56), channel_id=1, replica_groups=mesh['rows'=16,'feat'=16] {'rows'}, use_global_device_ids=true, to_apply=%region_4.4 | all-reduce | flops 8192 | bytes 65536 | tf_op jit(solution)/shard_map/while/body/eval_jaxpr/psum | solution.py:26
  1437.5 7.2 collective-permute-done.1
  1446.6 45.7 %psum.31 = f32[8,1024]{1,0:T(8,128)S(1)} all-reduce(f32[8,1024]{1,0:T(8,128)S(1)} %fusion.56), channel_id=1, replica_groups=mesh['rows'=16,'feat'=16] {'rows'}, use_global_device_ids=true, to_apply=%region_4.4 | all-reduce | flops 8192 | bytes 65536 | tf_op jit(solution)/shard_map/while/body/eval_jaxpr/psum | solution.py:26
  1497.4 7.2 collective-permute-done.1
  1506.6 45.7 %psum.31 = f32[8,1024]{1,0:T(8,128)S(1)} all-reduce(f32[8,1024]{1,0:T(8,128)S(1)} %fusion.56), channel_id=1, replica_groups=mesh['rows'=16,'feat'=16] {'rows'}, use_global_device_ids=true, to_apply=%region_4.4 | all-reduce | flops 8192 | bytes 65536 | tf_op jit(solution)/shard_map/while/body/eval_jaxpr/psum | solution.py:26
  1557.4 7.2 collective-permute-done.1
  1566.6 45.7 %psum.31 = f32[8,1024]{1,0:T(8,128)S(1)} all-reduce(f32[8,1024]{1,0:T(8,128)S(1)} %fusion.56), channel_id=1, replica_groups=mesh['rows'=16,'feat'=16] {'rows'}, use_global_device_ids=true, to_apply=%region_4.4 | all-reduce | flops 8192 | bytes 65536 | tf_op jit(solution)/shard_map/while/body/eval_jaxpr/psum | solution.py:26
  1617.4 7.2 collective-permute-done.1
  1626.6 45.7 %psum.31 = f32[8,1024]{1,0:T(8,128)S(1)} all-reduce(f32[8,1024]{1,0:T(8,128)S(1)} %fusion.56), channel_id=1, replica_groups=mesh['rows'=16,'feat'=16] {'rows'}, use_global_device_ids=true, to_apply=%region_4.4 | all-reduce | flops 8192 | bytes 65536 | tf_op jit(solution)/shard_map/while/body/eval_jaxpr/psum | solution.py:26
  1677.4 7.2 collective-permute-done.1
  1686.6 45.7 %psum.31 = f32[8,1024]{1,0:T(8,128)S(1)} all-reduce(f32[8,1024]{1,0:T(8,128)S(1)} %fusion.56), channel_id=1, replica_groups=mesh['rows'=16,'feat'=16] {'rows'}, use_global_device_ids=true, to_apply=%region_4.4 | all-reduce | flops 8192 | bytes 65536 | tf_op jit(solution)/shard_map/while/body/eval_jaxpr/psum | solution.py:26
  1737.4 7.2 collective-permute-done.1
  1746.6 45.7 %psum.31 = f32[8,1024]{1,0:T(8,128)S(1)} all-reduce(f32[8,1024]{1,0:T(8,128)S(1)} %fusion.56), channel_id=1, replica_groups=mesh['rows'=16,'feat'=16] {'rows'}, use_global_device_ids=true, to_apply=%region_4.4 | all-reduce | flops 8192 | bytes 65536 | tf_op jit(solution)/shard_map/while/body/eval_jaxpr/psum | solution.py:26
  1797.4 7.2 collective-permute-done.1
  1806.6 45.7 %psum.31 = f32[8,1024]{1,0:T(8,128)S(1)} all-reduce(f32[8,1024]{1,0:T(8,128)S(1)} %fusion.56), channel_id=1, replica_groups=mesh['rows'=16,'feat'=16] {'rows'}, use_global_device_ids=true, to_apply=%region_4.4 | all-reduce | flops 8192 | bytes 65536 | tf_op jit(solution)/shard_map/while/body/eval_jaxpr/psum | solution.py:26
  1857.4 7.2 collective-permute-done.1
  1866.6 45.7 %psum.31 = f32[8,1024]{1,0:T(8,128)S(1)} all-reduce(f32[8,1024]{1,0:T(8,128)S(1)} %fusion.56), channel_id=1, replica_groups=mesh['rows'=16,'feat'=16] {'rows'}, use_global_device_ids=true, to_apply=%region_4.4 | all-reduce | flops 8192 | bytes 65536 | tf_op jit(solution)/shard_map/while/body/eval_jaxpr/psum | solution.py:26
  (231 shorter events, 241.7 us)
Async XLA Ops:
  52.6 4.4 copy-start
  57.7 7.3 collective-permute-start
  112.6 4.4 copy-start
  117.7 7.3 collective-permute-start
  172.6 4.4 copy-start
  177.6 7.3 collective-permute-start
  232.6 4.4 copy-start
  237.6 7.3 collective-permute-start
  292.6 4.4 copy-start
  297.6 7.3 collective-permute-start
  352.5 4.4 copy-start
  357.6 7.3 collective-permute-start
  412.5 4.4 copy-start
  417.6 7.3 collective-permute-start
  472.5 4.4 copy-start
  477.6 7.3 collective-permute-start
  532.5 4.4 copy-start
  537.6 7.3 collective-permute-start
  592.5 4.4 copy-start
  597.6 7.3 collective-permute-start
  652.5 4.4 copy-start
  657.6 7.3 collective-permute-start
  712.5 4.4 copy-start
  717.5 7.3 collective-permute-start
  772.5 4.4 copy-start
  777.5 7.3 collective-permute-start
  832.5 4.4 copy-start
  837.5 7.3 collective-permute-start
  892.5 4.4 copy-start
  897.5 7.3 collective-permute-start
  952.4 4.4 copy-start
  957.5 7.3 collective-permute-start
  1012.4 4.4 copy-start.1
  1017.5 7.3 collective-permute-start.1
  1072.4 4.4 copy-start.1
  1077.5 7.3 collective-permute-start.1
  1132.4 4.4 copy-start.1
  1137.5 7.3 collective-permute-start.1
  1192.4 4.4 copy-start.1
  1197.5 7.3 collective-permute-start.1
  1252.4 4.4 copy-start.1
  1257.5 7.3 collective-permute-start.1
  1312.4 4.4 copy-start.1
  1317.4 7.3 collective-permute-start.1
  1372.4 4.4 copy-start.1
  1377.4 7.3 collective-permute-start.1
  1432.4 4.4 copy-start.1
  1437.4 7.3 collective-permute-start.1
  1492.3 4.4 copy-start.1
  1497.4 7.3 collective-permute-start.1
  1552.3 4.4 copy-start.1
  1557.4 7.3 collective-permute-start.1
  1612.3 4.4 copy-start.1
  1617.4 7.3 collective-permute-start.1
  1672.3 4.4 copy-start.1
  1677.4 7.3 collective-permute-start.1
  1732.3 4.4 copy-start.1
  1737.4 7.3 collective-permute-start.1
  1792.3 4.4 copy-start.1
  1797.4 7.3 collective-permute-start.1
  1852.3 4.4 copy-start.1
  1857.3 7.3 collective-permute-start.1
  1912.3 4.4 copy-start.1
  1917.3 7.3 collective-permute-start.1
  (1 other events, 0.8 us)
where the time goes:
time: 1930 us
  blocking collectives  1470 us (76%)
  waiting for transfers between devices  229 us (12%)
  matrix products  225 us (12%)
    psum x32, blocking collectives, refine(): projection = lax.psum(partial_value, 'rows')  1470 us
    ppermute x32, waiting for transfers between devices, passed_along(): return lax.ppermute(block, axis, route)  229 us
    dot_general x32, matrix products, refine(): jnp.dot(projection - ridge_weight * panel_weights, inverse_gram, precisio...  141 us
    dot_general x32, matrix products, refine(): jnp.dot(panel_rows.astype(jnp.bfloat16), features, preferred_element_type...  63.1 us
  transfers between devices with their start and end apart: 32, of which 32 were waited for; matrix products, arithmetic and copies ran while one was open for 0% of the time, Pallas kernels for 0%

commit v1 on v0

--- a/solution.py
+++ b/solution.py
@@ -23,7 +23,11 @@
         partial_value = jnp.dot(
             panel_rows.astype(jnp.bfloat16), features, preferred_element_type=jnp.float32
         )
-        projection = lax.psum(partial_value, "rows")
+        projection = partial_value
+        for hop in (1, 2, 4, 8):
+            projection = projection + lax.ppermute(
+                projection, "rows", [(dev, dev ^ hop) for dev in range(16)]
+            )
         increment = jnp.dot(
             projection - ridge_weight * panel_weights, inverse_gram, precision=lax.Precision.HIGHEST
         )

time: 1930 us -> 1030 us (0.53)
  blocking collectives: 1470 us -> 0 us
  waiting for transfers between devices: 229 us -> 638 us
  starting transfers between devices: 1.67 us -> 162 us
    psum x32 -> x0, blocking collectives: 1470 us -> none  [refine(): projection = lax.psum(partial_value, 'rows')]
    ppermute x0 -> x128, waiting for transfers between devices: none -> 408 us  [refine(): lax.ppermute(projection, 'rows', [(dev, dev ^ hop) for dev in range(16)])]
    ppermute x0 -> x128, starting transfers between devices: none -> 161 us  [refine(): lax.ppermute(projection, 'rows', [(dev, dev ^ hop) for dev in range(16)])]
  transfers between devices with their start and end apart: 32 -> 160, of which waited for: 32 -> 160; matrix products, arithmetic and copies ran while one was open for 0% -> 0% of each run, Pallas kernels for 0% -> 0%
where the time goes in v1:
time: 1030 us
  waiting for transfers between devices  638 us (62%)
  matrix products  225 us (22%)
  starting transfers between devices  162 us (16%)
    ppermute x128, waiting for transfers between devices, refine(): lax.ppermute(projection, 'rows', [(dev, dev ^ hop) for dev in range(16)])  408 us
    ppermute x32, waiting for transfers between devices, passed_along(): return lax.ppermute(block, axis, route)  230 us
    ppermute x128, starting transfers between devices, refine(): lax.ppermute(projection, 'rows', [(dev, dev ^ hop) for dev in range(16)])  161 us
    dot_general x32, matrix products, refine(): jnp.dot(projection - ridge_weight * panel_weights, inverse_gram, precisio...  141 us
    dot_general x32, matrix products, refine(): jnp.dot(panel_rows.astype(jnp.bfloat16), features, preferred_element_type...  63.1 us
  transfers between devices with their start and end apart: 160, of which 160 were waited for; matrix products, arithmetic and copies ran while one was open for 0% of the time, Pallas kernels for 0%

profile of v1, /device:TPU:0, one launch (start us, length us, event | category | flops | bytes accessed | tf_op | source)
XLA Modules:
  0.0 1029.8 jit_solution(11042574814025562035)
XLA Ops:
  1.4 514.4 %while.34 = (s32[]{:T(128)}, f32[8,1024]{1,0:T(8,128)S(1)}, f32[128,1024]{1,0:T(8,128)S(1)}, bf16[1024,1024]{1,0:T(8,128)(2,1)}, s32[]{:T(128)}, /*index=5*/f32[...) while((s32[]{:T(128)}, f32[8,1024]{1,0:T(8,128)S(1)}, ...), condition=%wide.region_1.2_spmd, body=%wide.region_0.1_spmd.sunk | while | flops 134299648 | bytes 18121224 | solution.py:59
  13.7 5.2 collective-permute-start.3
  21.6 4.4 fusion.51
  27.5 6.4 collective-permute-done.4
  46.1 4.9 collective-permute-start.3
  53.9 4.4 fusion.51
  59.0 7.2 collective-permute-done.4
  78.2 4.9 collective-permute-start.3
  91.1 7.2 collective-permute-done.4
  110.2 4.8 collective-permute-start.3
  123.2 7.2 collective-permute-done.4
  142.3 4.8 collective-permute-start.3
  155.2 7.2 collective-permute-done.4
  174.4 4.8 collective-permute-start.3
  187.3 7.2 collective-permute-done.4
  206.5 4.8 collective-permute-start.3
  214.7 4.4 fusion.51
  219.8 7.2 collective-permute-done.4
  238.9 4.5 collective-permute-start.3
  247.0 4.4 fusion.51
  252.1 7.2 collective-permute-done.4
  279.0 4.4 fusion.51
  284.1 7.2 collective-permute-done.4
  311.1 4.4 fusion.51
  316.2 7.2 collective-permute-done.4
  348.3 7.2 collective-permute-done.4
  375.3 4.4 fusion.51
  380.3 7.2 collective-permute-done.4
  407.3 4.4 fusion.51
  412.4 7.2 collective-permute-done.4
  444.5 7.2 collective-permute-done.4
  471.5 4.4 fusion.51
  476.5 7.2 collective-permute-done.4
  503.5 4.4 fusion.51
  508.6 7.2 collective-permute-done.4
  515.8 513.1 %while.35 = (s32[]{:T(128)}, f32[8,1024]{1,0:T(8,128)S(1)}, f32[128,1024]{1,0:T(8,128)S(1)}, bf16[1024,1024]{1,0:T(8,128)(2,1)}, s32[]{:T(128)}, /*index=5*/f32[...) while((s32[]{:T(128)}, f32[8,1024]{1,0:T(8,128)S(1)}, ...), condition=%wide.region_3.4_spmd, body=%wide.region_2.3_spmd.sunk | while | flops 134299648 | bytes 18121236 | solution.py:59
  535.6 4.4 fusion.59
  540.7 7.2 collective-permute-done.9
  567.7 4.4 fusion.59
  572.8 7.2 collective-permute-done.9
  604.8 7.2 collective-permute-done.9
  631.8 4.4 fusion.59
  636.9 7.2 collective-permute-done.9
  663.9 4.4 fusion.59
  669.0 7.2 collective-permute-done.9
  695.9 4.4 fusion.59
  701.0 7.2 collective-permute-done.9
  728.0 4.4 fusion.59
  733.1 7.2 collective-permute-done.9
  760.1 4.4 fusion.59
  765.2 7.2 collective-permute-done.9
  792.2 4.4 fusion.59
  797.2 7.2 collective-permute-done.9
  824.2 4.4 fusion.59
  829.3 7.2 collective-permute-done.9
  856.3 4.4 fusion.59
  861.4 7.2 collective-permute-done.9
  888.4 4.4 fusion.59
  893.5 7.2 collective-permute-done.9
  920.4 4.4 fusion.59
  925.5 7.2 collective-permute-done.9
  957.6 7.2 collective-permute-done.9
  989.7 7.2 collective-permute-done.9
  1021.7 7.2 collective-permute-done.9
  (551 shorter events, 662.3 us)
Async XLA Ops:
  13.7 7.8 collective-permute-start.3
  26.6 7.3 collective-permute-start.4
  46.1 7.8 collective-permute-start.3
  59.0 7.3 collective-permute-start.4
  78.2 7.8 collective-permute-start.3
  91.1 7.3 collective-permute-start.4
  110.2 7.8 collective-permute-start.3
  123.1 7.3 collective-permute-start.4
  142.3 7.8 collective-permute-start.3
  155.2 7.3 collective-permute-start.4
  174.4 7.8 collective-permute-start.3
  187.3 7.3 collective-permute-start.4
  206.5 8.2 collective-permute-start.3
  219.7 7.3 collective-permute-start.4
  238.9 8.1 collective-permute-start.3
  252.0 7.3 collective-permute-start.4
  271.2 7.8 collective-permute-start.3
  284.1 7.3 collective-permute-start.4
  303.3 7.8 collective-permute-start.3
  316.2 7.3 collective-permute-start.4
  335.4 7.8 collective-permute-start.3
  348.2 7.3 collective-permute-start.4
  367.4 7.8 collective-permute-start.3
  380.3 7.3 collective-permute-start.4
  399.5 7.8 collective-permute-start.3
  412.4 7.3 collective-permute-start.4
  431.6 7.8 collective-permute-start.3
  444.5 7.3 collective-permute-start.4
  463.6 7.8 collective-permute-start.3
  476.5 7.3 collective-permute-start.4
  495.7 7.8 collective-permute-start.3
  508.6 7.3 collective-permute-start.4
  527.8 7.8 collective-permute-start.8
  540.7 7.3 collective-permute-start.9
  559.8 7.8 collective-permute-start.8
  572.7 7.3 collective-permute-start.9
  591.9 7.8 collective-permute-start.8
  604.8 7.3 collective-permute-start.9
  624.0 7.8 collective-permute-start.8
  636.9 7.3 collective-permute-start.9
  656.1 7.8 collective-permute-start.8
  668.9 7.3 collective-permute-start.9
  688.1 7.8 collective-permute-start.8
  701.0 7.3 collective-permute-start.9
  720.2 7.8 collective-permute-start.8
  733.1 7.3 collective-permute-start.9
  752.3 7.8 collective-permute-start.8
  765.1 7.3 collective-permute-start.9
  784.3 7.8 collective-permute-start.8
  797.2 7.3 collective-permute-start.9
  816.4 7.8 collective-permute-start.8
  829.3 7.3 collective-permute-start.9
  848.5 7.8 collective-permute-start.8
  861.4 7.3 collective-permute-start.9
  880.5 7.8 collective-permute-start.8
  893.4 7.3 collective-permute-start.9
  912.6 7.8 collective-permute-start.8
  925.5 7.3 collective-permute-start.9
  944.7 7.8 collective-permute-start.8
  957.6 7.3 collective-permute-start.9
  976.7 7.8 collective-permute-start.8
  989.6 7.3 collective-permute-start.9
  1008.8 7.8 collective-permute-start.8
  1021.7 7.3 collective-permute-start.9
  (129 other events, 461.0 us)
